TPU v7x, 32 devices: a whole 2x2x4 slice. The times are simulated.
32 devices in a mesh: ch: 4 (over y, x), row: 8 (over z, core).
Axes of the slice: x: 2, y: 2, z: 4, core: 2. Of those that a mesh axis runs over, the one named last changes fastest.
Arguments:
- latent: bfloat16 [128, 32, 1280], P('row', None, 'ch'), may hold values from -50 to 50
- timestep: int32 [4], replicated, may hold values from 0 to 999
- norm_gain_a: float32 [1280], P('ch'), may hold values from 0.1 to 1.9
- conv_weight_a: bfloat16 [1280, 3, 3, 1280], P('ch'), may hold values from -0.0546875 to 0.0546875
- time_weight: bfloat16 [320, 1280], P(None, 'ch'), may hold values from -0.3125 to 0.3125
- norm_gain_b: float32 [1280], P('ch'), may hold values from 0.1 to 1.9
- conv_weight_b: bfloat16 [1280, 3, 3, 1280], P('ch'), may hold values from -0.0546875 to 0.0546875
- norm_gain_c: float32 [1280], P('ch'), may hold values from 0.1 to 1.9
- w_query: bfloat16 [1024, 1280], P('ch'), may hold values from -4 to 4
- w_key: bfloat16 [1024, 1280], P('ch'), may hold values from -4 to 4
- w_value: bfloat16 [1024, 1280], P('ch'), may hold values from -0.3125 to 0.3125
- w_out: bfloat16 [1280, 1024], P('ch'), may hold values from -0.1875 to 0.1875
Outputs:
- result: bfloat16 [128, 32, 1280], P('row', None, 'ch')
All inputs are finite; a program needn't handle non-finite values.
Results may differ from a plain program's by a relative error of at most 0.017.
Values may be sent and summed in bfloat16 or wider, within the bound.
A program may use at most 64 MiB of HBM per device.

v0:
```python
import math
import jax
import jax.numpy as jnp
from jax import lax
from jax.sharding import PartitionSpec as P

C = 1280
GROUPS = 32
HEAD_DIM = 64
TDIM = 320
H = 32
eps_value = 1e-06


def swapped(value, axis, stride):
    mask = 2**stride
    pairs = [(source, source ^ mask) for source in range(lax.axis_size(axis))]
    return lax.ppermute(value, axis, pairs)


def right_product(left, weight):
    return lax.dot_general(
        left, weight, (((1,), (1,)), ((), ())), preferred_element_type=jnp.float32
    )


def conv_taps(padded, weight):
    outcome = lax.conv_general_dilated(
        padded[None],
        weight,
        (1, 1),
        "VALID",
        dimension_numbers=("NHWC", "OHWI", "NHWC"),
        preferred_element_type=jnp.float32,
    )
    return outcome[0]


def pad_columns(field):
    return jnp.pad(field, ((0, 0), (1, 1), (0, 0)))


def body(
    latent,
    timestep,
    norm_gain_a,
    conv_weight_a,
    time_weight,
    norm_gain_b,
    conv_weight_b,
    norm_gain_c,
    w_query,
    w_key,
    w_value,
    w_out,
):
    rows, width, local_ch = latent.shape
    span = H // rows
    place = lax.axis_index("row")
    within = place % span
    image_id = place // span
    group_width = C // GROUPS
    local_groups = local_ch // group_width
    members = float(H * width * group_width)
    tokens = rows * width

    def group_norm(value, gain):
        flat = value.reshape(tokens, local_groups, group_width)
        stats = jnp.stack([jnp.sum(flat, axis=(0, 2)), jnp.sum(flat * flat, axis=(0, 2))])
        stats = stats + swapped(stats, "row", 0)
        mean = stats[0] / members
        spread = stats[1] / members - mean * mean
        scaled = (flat - mean[None, :, None]) * lax.rsqrt(spread + eps_value)[None, :, None]
        return scaled.reshape(rows, width, local_ch) * gain

    upper_half = within == 0

    def facing_row(field):
        return jnp.where(upper_half, field[-1:], field[:1])

    def attach_rim(field, partner):
        empty_row = jnp.zeros_like(partner)
        above = jnp.where(upper_half, empty_row, partner)
        below = jnp.where(upper_half, partner, empty_row)
        return jnp.concatenate([above, field, below], axis=0)

    def convolve(active, weight):
        full = lax.all_gather(active, "ch", axis=2, tiled=True)
        partner = swapped(facing_row(full), "row", 0)
        rimmed = attach_rim(full, partner)
        result_conv = conv_taps(pad_columns(rimmed), weight)
        return result_conv

    image_ids = jnp.arange(timestep.shape[0])
    step_value = jnp.sum(jnp.where(image_ids == image_id, timestep, 0)).astype(jnp.float32)
    half = TDIM // 2
    freqs = jnp.exp(-math.log(10000.0) * jnp.arange(half, dtype=jnp.float32) / half)
    angles = step_value * freqs
    sinus = jnp.concatenate([jnp.cos(angles), jnp.sin(angles)])[None, :].astype(jnp.bfloat16)
    time_add = jax.nn.silu(jnp.dot(sinus, time_weight, preferred_element_type=jnp.float32))
    source = latent.astype(jnp.float32)
    active_a = jax.nn.silu(group_norm(source, norm_gain_a)).astype(jnp.bfloat16)
    hidden_a = convolve(active_a, conv_weight_a) + time_add[None]
    active_b = jax.nn.silu(group_norm(hidden_a, norm_gain_b)).astype(jnp.bfloat16)
    hidden_b = source + convolve(active_b, conv_weight_b)
    normed = group_norm(hidden_b, norm_gain_c).astype(jnp.bfloat16).reshape(tokens, local_ch)
    inner = w_query.shape[0]
    projections = jnp.concatenate([w_query, w_key, w_value], axis=0)
    weight_cols = projections
    mixed = right_product(lax.all_gather(normed, "ch", axis=1, tiled=True), weight_cols)
    query = mixed[:, :inner].astype(jnp.bfloat16)
    keyed = mixed[:, inner : 2 * inner].astype(jnp.bfloat16)
    valued = mixed[:, 2 * inner :].astype(jnp.bfloat16)
    key_value = jnp.stack([keyed, valued])
    key_value = jnp.concatenate([key_value, swapped(key_value, "row", 0)], axis=1)
    local_heads = inner // HEAD_DIM
    query_heads = query.reshape(tokens, local_heads, HEAD_DIM)
    key_heads = key_value[0].reshape(-1, local_heads, HEAD_DIM)
    value_heads = key_value[1].reshape(-1, local_heads, HEAD_DIM)
    scores = jnp.einsum(
        "qhd,khd->hqk", query_heads, key_heads, preferred_element_type=jnp.float32
    ) * (1.0 / math.sqrt(HEAD_DIM))
    highest = jnp.max(scores, axis=-1, keepdims=True)
    raised = jnp.exp(scores - highest)
    weights = (raised / jnp.sum(raised, axis=-1, keepdims=True)).astype(jnp.bfloat16)
    heads_out = jnp.einsum("hqk,khd->qhd", weights, value_heads, preferred_element_type=jnp.float32)
    heads_out = heads_out.astype(jnp.bfloat16).reshape(tokens, inner)
    weight_cols = w_out
    projected = right_product(lax.all_gather(heads_out, "ch", axis=1, tiled=True), weight_cols)
    total = hidden_b.reshape(tokens, local_ch) + projected
    return total.reshape(rows, width, local_ch).astype(jnp.bfloat16)


def solution(mesh):
    return jax.shard_map(
        body,
        mesh=mesh,
        in_specs=(
            P("row", None, "ch"),
            P(),
            P("ch"),
            P("ch", None, None, None),
            P(None, "ch"),
            P("ch"),
            P("ch", None, None, None),
            P("ch"),
            P("ch", None),
            P("ch", None),
            P("ch", None),
            P("ch", None),
        ),
        out_specs=P("row", None, "ch"),
        check_vma=False,
    )
```

profile of v0, /device:TPU:0, one launch (start us, length us, event | category | flops | bytes accessed | tf_op | source)
XLA Modules:
  0.0 277.8 jit_solution(7291214916432832792)
XLA Ops:
  6.5 1.3 convert_reduce_fusion
  8.8 0.8 collective-permute-done
  9.9 1.3 fusion.55
  11.2 1.8 copy.96
  14.7 62.4 %all-gather.5.cloned.1.call-done = bf16[16,32,1280]{1,0,2:T(8,128)(2,1)} async-done(((bf16[16,32,320]{1,0,2:T(8,128)(2,1)}), bf16[16,32,1280]{1,0,2:T(8,128)(2,1)}) %all-gather.5.cloned.1.call-update) | async-done | bytes 1310736 | tf_op jit(solution)/shard_map/all_gather | solution.py:88
  77.1 3.0 %broadcast_select_fusion.5 = bf16[1,32,1280]{1,0,2:T(2,128)(2,1)S(1)} fusion(pred[]{:T(512)S(6)} %eq.11, bf16[16,32,1280]{1,0,2:T(8,128)(2,1)} %all-gather.5.cloned.1.call-done), kind=kLoop, calls=%fused_computation.48 | loop fusion | flops 40960 | bytes 245761 | tf_op jit(solution)/shard_map/jit(_where)/select_n | solution.py:79
  80.6 6.0 %copy.101 = bf16[16,32,1280]{2,1,0:T(8,128)(2,1)S(1)} copy(bf16[16,32,1280]{1,0,2:T(8,128)(2,1)} %all-gather.5.cloned.1.call-done) | data formatting | bytes 2621440 | tf_op jit(solution)/shard_map/all_gather | solution.py:88
  87.1 1.9 broadcast_select_fusion.4
  89.0 1.3 copy.100
  92.3 1.1 slice-done
  93.5 1.1 slice-done.1
  94.5 7.8 %select_reduce_fusion.1 = (f32[320]{0:T(512)S(1)}, f32[320]{0:T(512)S(1)}, f32[16,8,5,320]{3,1,2,0:T(8,128)S(1)}) fusion(f32[320]{0:T(512)S(1)} %divide_multiply_fusion, pred[8,5]{0,1:T(8,128)(4,1)S(1)} %copy-done.8, bf16[320,3,3,1280]{3,0,2,1:T(8,128)(2,1)S(1)} %bitcast.121, bf16[18,1,7,2,1280]{4,2,3,0,1:T(8,128)(2,1)S(1)} %slice.69, ...), kind=kOutput, calls=%fused_computation.59 | convolution fusion | flops 4727766016 | bytes 10684200 | tf_op jit(solution)/shard_map/conv_general_dilated | solution.py:28
  104.8 2.0 copy.107
  106.8 61.4 %all-gather.7.cloned.1.call-done = bf16[16,32,1280]{1,0,2:T(8,128)(2,1)} async-done(((bf16[16,32,320]{1,0,2:T(8,128)(2,1)}), bf16[16,32,1280]{1,0,2:T(8,128)(2,1)}) %all-gather.7.cloned.1.call-update) | async-done | bytes 1310736 | tf_op jit(solution)/shard_map/all_gather | solution.py:88
  168.2 3.0 %broadcast_select_fusion.2 = bf16[1,32,1280]{1,0,2:T(2,128)(2,1)S(1)} fusion(pred[]{:T(512)S(6)} %eq.11, bf16[16,32,1280]{1,0,2:T(8,128)(2,1)} %all-gather.7.cloned.1.call-done), kind=kLoop, calls=%fused_computation.45 | loop fusion | flops 40960 | bytes 245761 | tf_op jit(solution)/shard_map/jit(_where)/select_n | solution.py:79
  171.7 6.0 %copy.112 = bf16[16,32,1280]{2,1,0:T(8,128)(2,1)S(1)} copy(bf16[16,32,1280]{1,0,2:T(8,128)(2,1)} %all-gather.7.cloned.1.call-done) | data formatting | bytes 2621440 | tf_op jit(solution)/shard_map/all_gather | solution.py:88
  178.2 1.9 broadcast_select_fusion.1
  180.1 1.3 copy.111
  181.7 0.6 fusion.29
  183.4 1.1 slice-done.2
  184.6 1.1 slice-done.3
  185.6 7.8 %fusion.35 = f32[16,8,5,320]{3,1,2,0:T(8,128)S(1)} fusion(bf16[320,3,3,1280]{3,0,2,1:T(8,128)(2,1)S(1)} %bitcast.123, bf16[18,1,7,2,1280]{4,2,3,0,1:T(8,128)(2,1)S(1)} %slice.73, bf16[18,1,8,5,1280]{4,2,3,0,1:T(8,128)(2,1)S(1)} %copy.116, pred[8,5]{0,1:T(8,128)(4,1)S(1)} %copy-done.8), kind=kOutput, calls=%fused_computation.49 | convolution fusion | flops 4726538240 | bytes 10680360 | tf_op jit(solution)/shard_map/conv_general_dilated | solution.py:28
  194.8 0.8 collective-permute-done.4
  196.2 0.9 copy.120
  197.2 28.8 %all-gather.9.cloned.1.call-done = bf16[512,1280]{0,1:T(8,128)(2,1)} async-done(((bf16[512,320]{0,1:T(8,128)(2,1)}), bf16[512,1280]{0,1:T(8,128)(2,1)}) %all-gather.9.cloned.1.call-update) | async-done | bytes 1310736 | tf_op jit(solution)/shard_map/all_gather | solution.py:110
  225.9 2.7 fusion.32
  229.0 1.7 collective-permute-done.5
  231.3 5.0 %fusion.81 = (f32[4,512]{1,0:T(4,128)S(1)}, f32[4,512,1024]{2,1,0:T(8,128)}) fusion(bf16[512,4,64]{0,2,1:T(8,128)(2,1)S(1)} %bitcast.106, bf16[1024,4,64]{0,2,1:T(8,128)(2,1)S(1)} %bitcast.104), kind=kOutput, calls=%fused_computation.118 | convolution fusion | flops 274727936 | bytes 9183232 | tf_op jit(solution)/shard_map/sub | solution.py:124
  236.4 5.5 %fusion.44 = bf16[4,64,512]{2,1,0:T(8,128)(2,1)} fusion(bf16[1024,4,64]{0,2,1:T(8,128)(2,1)S(1)} %bitcast.105, f32[4,512,1024]{2,1,0:T(8,128)} %get-tuple-element.23, f32[4,512]{1,0:T(4,128)S(1)} %get-tuple-element.22), kind=kOutput, calls=%fused_computation.55 | convolution fusion | flops 272760832 | bytes 9183232 | tf_op jit(solution)/shard_map/hqk,khd->qhd/dot_general | solution.py:126
  242.5 26.1 %all-gather.11.cloned.1.call-done = bf16[512,1024]{0,1:T(8,128)(2,1)} async-done(((bf16[512,256]{0,1:T(8,128)(2,1)}), bf16[512,1024]{0,1:T(8,128)(2,1)}) %all-gather.11.cloned.1.call-update) | async-done | bytes 1048592 | tf_op jit(solution)/shard_map/all_gather | solution.py:129
  268.6 1.7 fusion.43
  270.3 0.9 copy.125
  (113 shorter events, 13.3 us)
Async XLA Ops:
  6.5 262.1 %copy-start = (bf16[320,1024]{1,0:T(8,128)(2,1)S(1)}, bf16[320,1024]{1,0:T(8,128)(2,1)}, u32[]{:S(2)}) copy-start(bf16[320,1024]{1,0:T(8,128)(2,1)} %param.23) | copy-start | bytes 1966084
  6.5 6.6 %copy-start.7 = (s32[4]{0:T(128)S(1)}, s32[4]{0:T(128)}, u32[]{:S(2)}) copy-start(s32[4]{0:T(128)} %param.13) | copy-start | bytes 52
  6.5 8.0 %copy-start.2 = (bf16[320,320]{1,0:T(8,128)(2,1)S(1)}, bf16[320,320]{1,0:T(8,128)(2,1)}, u32[]{:S(2)}) copy-start(bf16[320,320]{1,0:T(8,128)(2,1)} %param.16) | copy-start | bytes 614404
  6.5 70.5 %all-gather.5.cloned.1.call-start = ((), (), s32[]{:S(2)}) async-start(), calls=%async_computation | async-start | bytes 6553600 | tf_op jit(solution)/shard_map/all_gather | solution.py:88
  8.2 1.4 collective-permute-start
  13.0 155.2 %all-gather.7.cloned.1.call-start = ((), (), s32[]{:S(2)}) async-start(), calls=%async_computation.1 | async-start | bytes 6553600 | tf_op jit(solution)/shard_map/all_gather | solution.py:88
  80.5 6.1 %collective-permute-start.1 = (bf16[1,32,1280]{2,1,0:T(8,128)(2,1)S(1)}, bf16[1,32,1280]{2,1,0:T(8,128)(2,1)S(1)}, u32[]{:S(2)}, u32[]{:S(2)}) collective-permute-start(bf16[1,32,1280]{2,1,0:T(8,128)(2,1)S(1)} %copy.97), channel_id=1, source_target_pairs={{0,1},{1,0},{2,3},{3,2},{4,5},{5,4},{6,7},{7,6},{8,9},{9,8},{10,11... | collective-permute-start | bytes 245768 | tf_op jit(solution)/shard_map/ppermute | solution.py:18
  91.3 2.2 slice-start
  91.6 2.9 %slice-start.1 = ((s8[7372800]{0:T(1024)(128)(4,1)}), s8[3178496]{0:T(1024)(128)(4,1)S(1)}, s32[]{:S(2)}) async-start(s8[7372800]{0:T(1024)(128)(4,1)} %bitcast.120), calls=%async_computation.5 | async-start | bytes 6356992
  91.8 2.7 copy-start.8
  94.5 10.0 %copy-start.3 = (f32[320]{0:T(512)S(1)}, f32[320]{0:T(512)}, u32[]{:S(2)}) copy-start(f32[320]{0:T(512)} %param.17) | copy-start | bytes 3844
  102.8 1.4 collective-permute-start.2
  106.8 119.2 %all-gather.9.cloned.1.call-start = ((), (), s32[]{:S(2)}) async-start(), calls=%async_computation.2 | async-start | bytes 1638400 | tf_op jit(solution)/shard_map/all_gather | solution.py:110
  171.6 6.1 %collective-permute-start.3 = (bf16[1,32,1280]{2,1,0:T(8,128)(2,1)S(1)}, bf16[1,32,1280]{2,1,0:T(8,128)(2,1)S(1)}, u32[]{:S(2)}, u32[]{:S(2)}) collective-permute-start(bf16[1,32,1280]{2,1,0:T(8,128)(2,1)S(1)} %copy.108), channel_id=1, source_target_pairs={{0,1},{1,0},{2,3},{3,2},{4,5},{5,4},{6,7},{7,6},{8,9},{9,8},{10,11... | collective-permute-start | bytes 245768 | tf_op jit(solution)/shard_map/ppermute | solution.py:18
  182.4 2.2 slice-start.2
  182.7 2.9 %slice-start.3 = ((s8[7372800]{0:T(1024)(128)(4,1)}), s8[3178496]{0:T(1024)(128)(4,1)S(1)}, s32[]{:S(2)}) async-start(s8[7372800]{0:T(1024)(128)(4,1)} %bitcast.122), calls=%async_computation.7 | async-start | bytes 6356992
  185.6 8.0 %copy-start.1 = (bf16[16,32,320]{2,1,0:T(8,128)(2,1)S(1)}, bf16[16,32,320]{2,1,0:T(8,128)(2,1)}, u32[]{:S(2)}) copy-start(bf16[16,32,320]{2,1,0:T(8,128)(2,1)} %param.12) | copy-start | bytes 983044
  193.4 2.6 copy-start.4
  193.6 32.3 %copy-start.5 = (bf16[256,1280]{1,0:T(8,128)(2,1)S(1)}, bf16[256,1280]{1,0:T(8,128)(2,1)}, u32[]{:S(2)}) copy-start(bf16[256,1280]{1,0:T(8,128)(2,1)} %param.22) | copy-start | bytes 1966084
  193.6 32.3 %copy-start.6 = (bf16[256,1280]{1,0:T(8,128)(2,1)S(1)}, bf16[256,1280]{1,0:T(8,128)(2,1)}, u32[]{:S(2)}) copy-start(bf16[256,1280]{1,0:T(8,128)(2,1)} %param.21) | copy-start | bytes 1966084
  194.3 1.4 collective-permute-start.4
  197.1 71.5 %all-gather.11.cloned.1.call-start = ((), (), s32[]{:S(2)}) async-start(), calls=%async_computation.3 | async-start | bytes 1310720 | tf_op jit(solution)/shard_map/all_gather | solution.py:129
  228.8 2.0 collective-permute-start.5
Sparse Core Ops, SparseCore 0:
  13.2 63.8 all-gather.4
  106.9 61.2 all-gather.6
  197.2 28.6 all-gather.8
  242.1 26.4 all-gather.10
where the time goes:
time: 278 us
  waiting for transfers between devices  183 us (66%)
  local copies, waits for them, and re-layouts  32 us (12%)
  matrix products  30.8 us (11%)
  other arithmetic  15.9 us (6%)
  between operations  14.3 us (5%)
    all_gather x2, waiting for transfers between devices, convolve(): full = lax.all_gather(active, 'ch', axis=2, tiled=True)  124 us
    all_gather x1, waiting for transfers between devices, body(): lax.all_gather(normed, 'ch', axis=1, tiled=True)  28.8 us
    all_gather x1, waiting for transfers between devices, body(): lax.all_gather(heads_out, 'ch', axis=1, tiled=True)  26.1 us
    conv_general_dilated x2, matrix products, conv_taps(): lax.conv_general_dilated(padded[None], weight, (1, 1), 'VALID', dimension...  15.6 us
    all_gather x2, local copies, waits for them, and re-layouts, convolve(): full = lax.all_gather(active, 'ch', axis=2, tiled=True)  12 us
    select_n x2, other arithmetic, facing_row(): return jnp.where(upper_half, field[-1:], field[:1])  6.06 us
  transfers between devices with their start and end apart: 10, of which 8 were waited for; matrix products, arithmetic and copies ran while one was open for 5% of the time, Pallas kernels for 0%

commit v1 on v0

--- a/solution.py
+++ b/solution.py
@@ -85,7 +85,24 @@
         return jnp.concatenate([above, field, below], axis=0)
 
     def convolve(active, weight):
-        full = lax.all_gather(active, "ch", axis=2, tiled=True)
+
+        def end_plate(at_axis, obj):
+            parts_n = lax.axis_size("ch")
+            block_list = []
+            for it in [*range(1, parts_n)]:
+                block_list.append((it - 1, it))
+            top = block_list + [(parts_n - 1, 0)]
+            row_out = obj
+            pieces_in = [row_out]
+            for _ in [*range(parts_n - 1)]:
+                row_out = lax.ppermute(row_out, "ch", top)
+                pieces_in += [row_out]
+            base_arr = jnp.concatenate([*reversed(pieces_in)], axis=at_axis)
+            before = lax.axis_index("ch")
+            oldest = jnp.roll(base_arr, (before + 1) * row_out.shape[at_axis], at_axis)
+            return oldest
+
+        full = end_plate(2, active)
         partner = swapped(facing_row(full), "row", 0)
         rimmed = attach_rim(full, partner)
         result_conv = conv_taps(pad_columns(rimmed), weight)

time: 278 us -> 201 us (0.72)
  waiting for transfers between devices: 183 us -> 124 us
  local copies, waits for them, and re-layouts: 32 us -> 13.9 us
  other arithmetic: 15.9 us -> 11.4 us
  starting transfers between devices: 2.01 us -> 5.17 us
    all_gather x2 -> x0, waiting for transfers between devices: 124 us -> none  [convolve(): full = lax.all_gather(active, 'ch', axis=2, tiled=True)]
    ppermute x0 -> x6, waiting for transfers between devices: none -> 62.3 us  [end_plate(): row_out = lax.ppermute(row_out, 'ch', top)]
    all_gather x2 -> x0, local copies, waits for them, and re-layouts: 12 us -> none  [convolve(): full = lax.all_gather(active, 'ch', axis=2, tiled=True)]
    select_n x2, other arithmetic: 6.06 us -> 0.52 us  [facing_row(): return jnp.where(upper_half, field[-1:], field[:1])]
    concatenate x0 -> x2, local copies, waits for them, and re-layouts: none -> 4.64 us  [end_plate(): base_arr = jnp.concatenate([*reversed(pieces_in)], axis=at_axis)]
    select_n x6 -> x0, local copies, waits for them, and re-layouts: 4.01 us -> none  [the longest x2 2.54 us: attach_rim(): above = jnp.where(upper_half, empty_row, partner)]
    convert_element_type x2 -> x0, local copies, waits for them, and re-layouts: 3.73 us -> none  [the longest x1 1.96 us: body(): jax.nn.silu(group_norm(hidden_a, norm_gain_b)).astype(jnp.bfloat16)]
    ppermute x0 -> x6, starting transfers between devices: none -> 3.72 us  [end_plate(): row_out = lax.ppermute(row_out, 'ch', top)]
  transfers between devices with their start and end apart: 10 -> 14, of which waited for: 8 -> 14; matrix products, arithmetic and copies ran while one was open for 5% -> 2% of each run, Pallas kernels for 0% -> 0%
where the time goes in v1:
time: 201 us
  waiting for transfers between devices  124 us (62%)
  matrix products  31.5 us (16%)
  between operations  14.5 us (7%)
  local copies, waits for them, and re-layouts  13.9 us (7%)
  other arithmetic  11.4 us (6%)
  starting transfers between devices  5.17 us (3%)
    ppermute x6, waiting for transfers between devices, end_plate(): row_out = lax.ppermute(row_out, 'ch', top)  62.3 us
    all_gather x1, waiting for transfers between devices, body(): lax.all_gather(normed, 'ch', axis=1, tiled=True)  28.5 us
    all_gather x1, waiting for transfers between devices, body(): lax.all_gather(heads_out, 'ch', axis=1, tiled=True)  26.1 us
    conv_general_dilated x2, matrix products, conv_taps(): lax.conv_general_dilated(padded[None], weight, (1, 1), 'VALID', dimension...  15.6 us
    ppermute x6, waiting for transfers between devices, swapped(): return lax.ppermute(value, axis, pairs)  7.16 us
    dot_general x1, matrix products, body(): jnp.einsum('hqk,khd->qhd', weights, value_heads, preferred_element_type=j...  5.55 us
    sub x1, matrix products, body(): raised = jnp.exp(scores - highest)  4.82 us
    concatenate x2, local copies, waits for them, and re-layouts, end_plate(): base_arr = jnp.concatenate([*reversed(pieces_in)], axis=at_axis)  4.64 us
  transfers between devices with their start and end apart: 14, of which 14 were waited for; matrix products, arithmetic and copies ran while one was open for 2% of the time, Pallas kernels for 0%

profile of v1, /device:TPU:0, one launch (start us, length us, event | category | flops | bytes accessed | tf_op | source)
XLA Modules:
  0.0 200.5 jit_solution(2828639947794651513)
XLA Ops:
  6.5 1.2 convert_reduce_fusion
  9.9 1.3 fusion.57
  11.2 2.9 %collective-permute-start.1 = (bf16[16,32,320]{2,0,1:T(8,128)(2,1)S(1)}, bf16[16,32,320]{2,0,1:T(8,128)(2,1)S(1)}, u32[]{:S(2)}, u32[]{:S(2)}) collective-permute-start(bf16[16,32,320]{2,0,1:T(8,128)(2,1)S(1)} %fusion.57), channel_id=1, source_target_pairs={{0,8},{8,16},{16,24},{24,0},{1,9},{9,17},{17,25},{25,1},{2,10},{10... | collective-permute-start | bytes 983048 | tf_op jit(solution)/shard_map/ppermute | solution.py:98
  14.1 10.4 %collective-permute-done.1 = bf16[16,32,320]{2,0,1:T(8,128)(2,1)S(1)} collective-permute-done((bf16[16,32,320]{2,0,1:T(8,128)(2,1)S(1)}, bf16[16,32,320]{2,0,1:T(8,128)(2,1)S(1)}, u32[]{:S(2)}, u32[]{:S(2)}) %collective-permute-start.1) | collective-permute-done | bytes 327712 | tf_op jit(solution)/shard_map/ppermute | solution.py:98
  25.3 1.3 fusion.62
  27.2 8.8 %collective-permute-done.2 = bf16[16,32,320]{2,0,1:T(8,128)(2,1)S(1)} collective-permute-done((bf16[16,32,320]{2,0,1:T(8,128)(2,1)S(1)}, bf16[16,32,320]{2,0,1:T(8,128)(2,1)S(1)}, u32[]{:S(2)}, u32[]{:S(2)}) %collective-permute-start.2) | collective-permute-done | bytes 327712 | tf_op jit(solution)/shard_map/ppermute | solution.py:98
  36.1 1.1 convolution_reduce_fusion
  37.3 9.4 %collective-permute-done.3 = bf16[16,32,320]{2,0,1:T(8,128)(2,1)S(1)} collective-permute-done((bf16[16,32,320]{2,0,1:T(8,128)(2,1)S(1)}, bf16[16,32,320]{2,0,1:T(8,128)(2,1)S(1)}, u32[]{:S(2)}, u32[]{:S(2)}) %collective-permute-start.3) | collective-permute-done | bytes 327712 | tf_op jit(solution)/shard_map/ppermute | solution.py:98
  46.6 2.1 %concatenate.27 = bf16[16,32,1280]{2,0,1:T(8,128)(2,1)S(1)} concatenate(bf16[16,32,320]{2,0,1:T(8,128)(2,1)S(1)} %collective-permute-done.3, bf16[16,32,320]{2,0,1:T(8,128)(2,1)S(1)} %collective-permute-done.2, bf16[16,32,320]{2,0,1:T(8,128)(2,1)S(1)} %collective-permute-done.1, bf16[16,32,320]{2,0,1:T(8,128)(2,1)S(1)} %fusion.57), dimensions={2} | concatenate | bytes 2621440 | tf_op jit(solution)/shard_map/concatenate | solution.py:100
  48.8 1.2 fusion.36
  50.3 1.4 collective-permute-done.4
  52.0 1.2 fusion.24
  54.2 1.2 slice-done.1
  55.4 7.8 %select_reduce_fusion.1 = (f32[320]{0:T(512)S(1)}, f32[320]{0:T(512)S(1)}, f32[16,8,5,320]{3,1,2,0:T(8,128)S(1)}) fusion(f32[320]{0:T(512)S(1)} %divide_multiply_fusion, pred[8,5]{0,1:T(8,128)(4,1)S(1)} %copy-done.6, bf16[320,3,3,1280]{3,0,2,1:T(8,128)(2,1)S(1)} %bitcast.121, bf16[18,1,7,2,1280]{4,2,3,0,1:T(8,128)(2,1)S(1)} %slice.69, ...), kind=kOutput, calls=%fused_computation.59 | convolution fusion | flops 4727766016 | bytes 10684200 | tf_op jit(solution)/shard_map/conv_general_dilated | solution.py:28
  65.6 12.1 %collective-permute-done.6 = bf16[16,32,320]{2,0,1:T(8,128)(2,1)S(1)} collective-permute-done((bf16[16,32,320]{2,0,1:T(8,128)(2,1)S(1)}, bf16[16,32,320]{2,0,1:T(8,128)(2,1)S(1)}, u32[]{:S(2)}, u32[]{:S(2)}) %collective-permute-start.6) | collective-permute-done | bytes 327712 | tf_op jit(solution)/shard_map/ppermute | solution.py:98
  77.7 11.2 %collective-permute-done.7 = bf16[16,32,320]{2,0,1:T(8,128)(2,1)S(1)} collective-permute-done((bf16[16,32,320]{2,0,1:T(8,128)(2,1)S(1)}, bf16[16,32,320]{2,0,1:T(8,128)(2,1)S(1)}, u32[]{:S(2)}, u32[]{:S(2)}) %collective-permute-start.7) | collective-permute-done | bytes 327712 | tf_op jit(solution)/shard_map/ppermute | solution.py:98
  88.9 10.5 %collective-permute-done.8 = bf16[16,32,320]{2,0,1:T(8,128)(2,1)} collective-permute-done((bf16[16,32,320]{2,0,1:T(8,128)(2,1)S(1)}, bf16[16,32,320]{2,0,1:T(8,128)(2,1)}, u32[]{:S(2)}, u32[]{:S(2)}) %collective-permute-start.8) | collective-permute-done | bytes 327712 | tf_op jit(solution)/shard_map/ppermute | solution.py:98
  99.4 2.5 %concatenate.30 = bf16[16,32,1280]{2,0,1:T(8,128)(2,1)S(1)} concatenate(bf16[16,32,320]{2,0,1:T(8,128)(2,1)} %collective-permute-done.8, bf16[16,32,320]{2,0,1:T(8,128)(2,1)S(1)} %collective-permute-done.7, bf16[16,32,320]{2,0,1:T(8,128)(2,1)S(1)} %collective-permute-done.6, bf16[16,32,320]{2,0,1:T(8,128)(2,1)S(1)} %multiply_convert_fusion.1), dimensions={2} | concatenate | bytes 2621440 | tf_op jit(solution)/shard_map/concatenate | solution.py:100
  101.9 1.2 fusion.35
  103.4 1.4 collective-permute-done.9
  105.1 1.2 fusion.23
  107.3 1.2 slice-done.3
  108.5 7.8 %fusion.37 = f32[16,8,5,320]{3,1,2,0:T(8,128)S(1)} fusion(bf16[320,3,3,1280]{3,0,2,1:T(8,128)(2,1)S(1)} %bitcast.123, bf16[18,1,7,2,1280]{4,2,3,0,1:T(8,128)(2,1)S(1)} %slice.73, bf16[18,1,8,5,1280]{4,2,3,0,1:T(8,128)(2,1)S(1)} %copy.65, pred[8,5]{0,1:T(8,128)(4,1)S(1)} %copy-done.6), kind=kOutput, calls=%fused_computation.49 | convolution fusion | flops 4726538240 | bytes 10680360 | tf_op jit(solution)/shard_map/conv_general_dilated | solution.py:28
  117.3 1.0 collective-permute-done.10
  120.1 28.5 %all-gather.3.cloned.1.call-done = bf16[512,1280]{0,1:T(8,128)(2,1)} async-done(((bf16[512,320]{0,1:T(8,128)(2,1)}), bf16[512,1280]{0,1:T(8,128)(2,1)}) %all-gather.3.cloned.1.call-update) | async-done | bytes 1310736 | tf_op jit(solution)/shard_map/all_gather | solution.py:127
  148.6 2.7 %fusion.32 = bf16[512,768]{1,0:T(8,128)(2,1)S(1)} fusion(bf16[512,1280]{0,1:T(8,128)(2,1)} %all-gather.3.cloned.1.call-done, bf16[256,1280]{1,0:T(8,128)(2,1)S(1)} %copy-done.4, bf16[256,1280]{1,0:T(8,128)(2,1)S(1)} %copy-done.5, bf16[256,1280]{1,0:T(8,128)(2,1)} %param.22), kind=kOutput, calls=%fused_computation.42 | convolution fusion | flops 1012924416 | bytes 4063232 | tf_op jit(solution)/shard_map/dot_general | solution.py:22
  151.6 1.7 collective-permute-done.11
  154.0 4.8 %fusion.83 = (f32[4,512]{1,0:T(4,128)S(1)}, f32[4,512,1024]{2,1,0:T(8,128)}) fusion(bf16[512,4,64]{0,2,1:T(8,128)(2,1)S(1)} %bitcast.106, bf16[1024,4,64]{0,2,1:T(8,128)(2,1)S(1)} %bitcast.104), kind=kOutput, calls=%fused_computation.124 | convolution fusion | flops 274727936 | bytes 9183232 | tf_op jit(solution)/shard_map/sub | solution.py:141
  158.8 5.5 %fusion.46 = bf16[4,64,512]{2,1,0:T(8,128)(2,1)} fusion(bf16[1024,4,64]{0,2,1:T(8,128)(2,1)S(1)} %bitcast.105, f32[4,512,1024]{2,1,0:T(8,128)} %get-tuple-element.24, f32[4,512]{1,0:T(4,128)S(1)} %get-tuple-element.23), kind=kOutput, calls=%fused_computation.55 | convolution fusion | flops 272760832 | bytes 9183232 | tf_op jit(solution)/shard_map/hqk,khd->qhd/dot_general | solution.py:143
  164.9 26.1 %all-gather.5.cloned.1.call-done = bf16[512,1024]{0,1:T(8,128)(2,1)} async-done(((bf16[512,256]{0,1:T(8,128)(2,1)}), bf16[512,1024]{0,1:T(8,128)(2,1)}) %all-gather.5.cloned.1.call-update) | async-done | bytes 1048592 | tf_op jit(solution)/shard_map/all_gather | solution.py:146
  191.0 1.7 fusion.45
  192.8 0.9 copy.74
  (105 shorter events, 12.6 us)
Async XLA Ops:
  6.5 184.5 %copy-start = (bf16[320,1024]{1,0:T(8,128)(2,1)S(1)}, bf16[320,1024]{1,0:T(8,128)(2,1)}, u32[]{:S(2)}) copy-start(bf16[320,1024]{1,0:T(8,128)(2,1)} %param.25) | copy-start | bytes 1966084
  6.5 142.0 %all-gather.3.cloned.1.call-start = ((), (), s32[]{:S(2)}) async-start(), calls=%async_computation | async-start | bytes 1638400 | tf_op jit(solution)/shard_map/all_gather | solution.py:127
  8.2 1.4 collective-permute-start
  11.2 13.3 %collective-permute-start.1 = (bf16[16,32,320]{2,0,1:T(8,128)(2,1)S(1)}, bf16[16,32,320]{2,0,1:T(8,128)(2,1)S(1)}, u32[]{:S(2)}, u32[]{:S(2)}) collective-permute-start(bf16[16,32,320]{2,0,1:T(8,128)(2,1)S(1)} %fusion.57), channel_id=1, source_target_pairs={{0,8},{8,16},{16,24},{24,0},{1,9},{9,17},{17,25},{25,1},{2,10},{10... | collective-permute-start | bytes 983048 | tf_op jit(solution)/shard_map/ppermute | solution.py:98
  24.5 11.5 %collective-permute-start.2 = (bf16[16,32,320]{2,0,1:T(8,128)(2,1)S(1)}, bf16[16,32,320]{2,0,1:T(8,128)(2,1)S(1)}, u32[]{:S(2)}, u32[]{:S(2)}) collective-permute-start(bf16[16,32,320]{2,0,1:T(8,128)(2,1)S(1)} %collective-permute-done.1), channel_id=1, source_target_pairs={{0,8},{8,16},{16,24},{24,0},{1,9},{9,17},{17,25},{25,1},{2,10},{10... | collective-permute-start | bytes 983048 | tf_op jit(solution)/shard_map/ppermute | solution.py:98
  36.0 10.6 %collective-permute-start.3 = (bf16[16,32,320]{2,0,1:T(8,128)(2,1)S(1)}, bf16[16,32,320]{2,0,1:T(8,128)(2,1)S(1)}, u32[]{:S(2)}, u32[]{:S(2)}) collective-permute-start(bf16[16,32,320]{2,0,1:T(8,128)(2,1)S(1)} %collective-permute-done.2), channel_id=1, source_target_pairs={{0,8},{8,16},{16,24},{24,0},{1,9},{9,17},{17,25},{25,1},{2,10},{10... | collective-permute-start | bytes 983048 | tf_op jit(solution)/shard_map/ppermute | solution.py:98
  50.3 1.5 collective-permute-start.4
  52.0 2.2 %slice-start = ((s8[7372800]{0:T(1024)(128)(4,1)}), s8[4194304]{0:T(1024)(128)(4,1)S(1)}, s32[]{:S(2)}) async-start(s8[7372800]{0:T(1024)(128)(4,1)} %bitcast.120), calls=%async_computation.2 | async-start | bytes 8388608
  53.2 2.2 %slice-start.1 = ((s8[7372800]{0:T(1024)(128)(4,1)}), s8[3178496]{0:T(1024)(128)(4,1)S(1)}, s32[]{:S(2)}) async-start(s8[7372800]{0:T(1024)(128)(4,1)} %bitcast.120), calls=%async_computation.3 | async-start | bytes 6356992
  53.4 2.0 %copy-start.6 = (pred[8,5]{0,1:T(8,128)(4,1)S(1)}, pred[8,5]{0,1:T(8,128)(4,1)}, u32[]{:S(2)}) copy-start(pred[8,5]{0,1:T(8,128)(4,1)} %constant.94) | copy-start | bytes 124
  55.4 9.8 %copy-start.2 = (f32[320]{0:T(512)S(1)}, f32[320]{0:T(512)}, u32[]{:S(2)}) copy-start(f32[320]{0:T(512)} %param.19) | copy-start | bytes 3844
  63.7 1.2 collective-permute-start.5
  65.5 12.1 %collective-permute-start.6 = (bf16[16,32,320]{2,0,1:T(8,128)(2,1)S(1)}, bf16[16,32,320]{2,0,1:T(8,128)(2,1)S(1)}, u32[]{:S(2)}, u32[]{:S(2)}) collective-permute-start(bf16[16,32,320]{2,0,1:T(8,128)(2,1)S(1)} %multiply_convert_fusion.1), channel_id=1, source_target_pairs={{0,8},{8,16},{16,24},{24,0},{1,9},{9,17},{17,25},{25,1},{2,10},{10... | collective-permute-start | bytes 983048 | tf_op jit(solution)/shard_map/ppermute | solution.py:98
  77.7 11.2 %collective-permute-start.7 = (bf16[16,32,320]{2,0,1:T(8,128)(2,1)S(1)}, bf16[16,32,320]{2,0,1:T(8,128)(2,1)S(1)}, u32[]{:S(2)}, u32[]{:S(2)}) collective-permute-start(bf16[16,32,320]{2,0,1:T(8,128)(2,1)S(1)} %collective-permute-done.6), channel_id=1, source_target_pairs={{0,8},{8,16},{16,24},{24,0},{1,9},{9,17},{17,25},{25,1},{2,10},{10... | collective-permute-start | bytes 983048 | tf_op jit(solution)/shard_map/ppermute | solution.py:98
  88.9 10.5 %collective-permute-start.8 = (bf16[16,32,320]{2,0,1:T(8,128)(2,1)S(1)}, bf16[16,32,320]{2,0,1:T(8,128)(2,1)}, u32[]{:S(2)}, u32[]{:S(2)}) collective-permute-start(bf16[16,32,320]{2,0,1:T(8,128)(2,1)S(1)} %collective-permute-done.7), channel_id=1, source_target_pairs={{0,8},{8,16},{16,24},{24,0},{1,9},{9,17},{17,25},{25,1},{2,10},{10... | collective-permute-start | bytes 983048 | tf_op jit(solution)/shard_map/ppermute | solution.py:98
  103.3 1.5 collective-permute-start.9
  105.1 2.2 %slice-start.2 = ((s8[7372800]{0:T(1024)(128)(4,1)}), s8[4194304]{0:T(1024)(128)(4,1)S(1)}, s32[]{:S(2)}) async-start(s8[7372800]{0:T(1024)(128)(4,1)} %bitcast.122), calls=%async_computation.4 | async-start | bytes 8388608
  106.3 2.2 %slice-start.3 = ((s8[7372800]{0:T(1024)(128)(4,1)}), s8[3178496]{0:T(1024)(128)(4,1)S(1)}, s32[]{:S(2)}) async-start(s8[7372800]{0:T(1024)(128)(4,1)} %bitcast.122), calls=%async_computation.5 | async-start | bytes 6356992
  108.5 8.0 %copy-start.1 = (bf16[16,32,320]{2,1,0:T(8,128)(2,1)S(1)}, bf16[16,32,320]{2,1,0:T(8,128)(2,1)}, u32[]{:S(2)}) copy-start(bf16[16,32,320]{2,1,0:T(8,128)(2,1)} %param.14) | copy-start | bytes 983044
  116.3 2.4 %copy-start.3 = (f32[320]{0:T(512)S(1)}, f32[320]{0:T(512)}, u32[]{:S(2)}) copy-start(f32[320]{0:T(512)} %param.21) | copy-start | bytes 3844
  116.5 32.1 %copy-start.4 = (bf16[256,1280]{1,0:T(8,128)(2,1)S(1)}, bf16[256,1280]{1,0:T(8,128)(2,1)}, u32[]{:S(2)}) copy-start(bf16[256,1280]{1,0:T(8,128)(2,1)} %param.24) | copy-start | bytes 1966084
  116.5 32.1 %copy-start.5 = (bf16[256,1280]{1,0:T(8,128)(2,1)S(1)}, bf16[256,1280]{1,0:T(8,128)(2,1)}, u32[]{:S(2)}) copy-start(bf16[256,1280]{1,0:T(8,128)(2,1)} %param.23) | copy-start | bytes 1966084
  117.1 1.2 collective-permute-start.10
  119.8 71.2 %all-gather.5.cloned.1.call-start = ((), (), s32[]{:S(2)}) async-start(), calls=%async_computation.1 | async-start | bytes 1310720 | tf_op jit(solution)/shard_map/all_gather | solution.py:146
  151.4 2.0 collective-permute-start.11
Sparse Core Ops, SparseCore 0:
  119.9 28.5 all-gather.2
  164.5 26.4 all-gather.4
